TPU v7x, 32 devices: a whole 2x2x4 slice. The times are simulated.
32 devices in a mesh: group: 2 (over x), module: 16 (over z, y, core).
Axes of the slice: x: 2, y: 2, z: 4, core: 2. Of those that a mesh axis runs over, the one named last changes fastest.
Arguments:
- query_grads: float32 [16, 32, 128, 128], P(None, None, 'module'), may hold values from -0.1875 to 0.1875
- train_grads: float32 [32, 128, 128, 128], P('module', 'group'), parts along dimension 1, may hold values from -0.1875 to 0.1875
- out_basis: float32 [32, 128, 128], P('module'), may hold values from -0.5 to 0.5
- in_basis: float32 [32, 128, 128], P('module'), may hold values from -0.5 to 0.5
- corrections: float32 [32, 128, 128], P('module'), may hold values from 0.01 to 10
- ranks: int32 [16], replicated, may hold values from 32 to 128
- slot_modules: int32 [32], replicated, may hold values from -1 to 15, as said below
Outputs:
- scores: float32 [32, 128], P(None, 'group'), parts along dimension 1
There are 2 independent parts, one for each index of `group`. A program takes and returns all parts, laid end to end along the dimension named above; an argument that names none is the same for every part. Nothing has to cross between parts.
Inputs may be any that keep to these rules, and one draw needn't show every extreme that they name: `slot_modules`: each module number 0 to 15 stands in exactly one entry; all other entries are -1. Owner i holds the 2 entries from i * 2 on, so an owner holds 0 to 2 modules, and some owner holds 2.
All inputs are finite; a program needn't handle non-finite values.
Results may differ from a plain program's by a relative error of at most 0.0003.
Values sent between devices are 32-bit elements; how exact they have to be, the bound alone decides.
No kernel may reach another device: no remote copies, remote signals or barrier semaphores. Data moves between devices by JAX's collectives and lax.ppermute only.
A program may use at most 128 MiB of HBM per device.

v0:
```python
import jax
import jax.numpy as jnp
from jax import lax
from jax.sharding import PartitionSpec as P


def rotate(field, output_eigenbasis, inner_basis):
    inner = jnp.einsum("noi,ib->nob", field, inner_basis, precision=lax.Precision.HIGHEST)
    return jnp.einsum("oa,nob->nab", output_eigenbasis, inner, precision=lax.Precision.HIGHEST)


def blank_rotation(field, output_eigenbasis, inner_basis):
    return jnp.zeros(field.shape, jnp.float32)


def slot_weight(spectrum, keep_rank):
    damping = 0.1 * jnp.mean(spectrum)
    positions = lax.iota(jnp.int32, spectrum.shape[0])
    kept_mask = (positions[:, None] < keep_rank) & (positions[None, :] < keep_rank)
    return jnp.where(kept_mask, 1.0 / (spectrum + damping), jnp.zeros_like(spectrum))


def score_rotated(query_block, rotated_train, output_eigenbasis, inner_basis, spectrum, keep_rank):
    scaled = rotate(query_block, output_eigenbasis, inner_basis) * slot_weight(spectrum, keep_rank)
    return jnp.einsum("qab,eab->qe", scaled, rotated_train, precision=lax.Precision.HIGHEST)


def blank_scores(query_block, second_block, output_eigenbasis, inner_basis, spectrum, keep_rank):
    return jnp.zeros((query_block.shape[0], second_block.shape[0]), jnp.float32)


def body(query_grads, train_grads, out_basis, in_basis, corrections, ranks, slot_modules):
    slot_count = out_basis.shape[0]
    peer_count = lax.axis_size("module")
    own_index = lax.axis_index("module")
    owned_modules = lax.dynamic_slice_in_dim(slot_modules, own_index * slot_count, slot_count)
    query_count = query_grads.shape[1]
    example_count = train_grads.shape[1]
    rotated = []
    for number in range(slot_count):
        rotated.append(
            lax.cond(
                owned_modules[number] >= 0,
                rotate,
                blank_rotation,
                train_grads[number],
                out_basis[number],
                in_basis[number],
            )
        )
    safe_index = jnp.maximum(slot_modules, 0)
    populated_slots = slot_modules >= 0
    outgoing = jnp.where(populated_slots[:, None, None, None], query_grads[safe_index], 0.0)
    outgoing = outgoing.reshape((peer_count, slot_count) + outgoing.shape[1:])
    received = lax.all_to_all(outgoing, "module", split_axis=0, concat_axis=3, tiled=True)[0]
    running = jnp.zeros((query_count, example_count), jnp.float32)
    for number in range(slot_count):
        module = owned_modules[number]
        keep_rank = ranks[jnp.maximum(module, 0)]
        term = lax.cond(
            module >= 0,
            score_rotated,
            blank_scores,
            received[number],
            rotated[number],
            out_basis[number],
            in_basis[number],
            corrections[number],
            keep_rank,
        )
        running = running + term
    return lax.psum(running, "module")


def solution(mesh):
    return jax.shard_map(
        body,
        mesh=mesh,
        in_specs=(
            P(None, None, "module", None),
            P("module", "group", None, None),
            P("module", None, None),
            P("module", None, None),
            P("module", None, None),
            P(),
            P(),
        ),
        out_specs=P(None, "group"),
        check_vma=False,
    )
```

profile of v0, /device:TPU:0, one launch (start us, length us, event | category | flops | bytes accessed | tf_op | source)
XLA Modules:
  0.0 223.0 jit_solution(18283808478415897497)
XLA Ops:
  0.0 0.0 copy-start
  0.0 0.8 broadcast_maximum_fusion
  0.8 0.7 broadcast_compare_fusion
  1.5 0.1 broadcast_in_dim.24
  1.6 0.0 copy-done
  1.6 2.8 %gather_fusion = f32[32,32,8,128]{3,2,1,0:T(8,128)} fusion(f32[16,32,8,128]{3,2,1,0:T(8,128)S(1)} %copy-done, s32[1024]{0:T(1024)S(1)} %pad_clamp_fusion), kind=kCustom, calls=%fused_computation | custom fusion | bytes 8388736 | tf_op jit(solution)/shard_map/gather | solution.py:53
  4.4 4.8 %broadcast_select_fusion = f32[16,2,32,8,128]{4,3,2,1,0:T(8,128)} fusion(f32[16,2,32,8,128]{4,3,2,1,0:T(8,128)} %bitcast.80, pred[16,2]{1,0:T(8,128)(4,1)S(1)} %broadcast_in_dim.24), kind=kLoop, calls=%fused_computation.37 | loop fusion | flops 1048576 | bytes 8388640 | tf_op jit(solution)/shard_map/jit(_where)/select_n | solution.py:53
  9.1 0.0 copy-start.4
  9.1 0.0 copy-start.2
  9.1 0.0 copy-start.3
  9.1 7.6 %all-to-all-start = ((f32[16,2,32,8,128]{4,3,2,1,0:T(8,128)}), f32[16,2,32,8,128]{4,3,2,1,0:T(8,128)}, u32[]{:S(2)}, u32[]{:S(2)}) async-start(f32[16,2,32,8,128]{4,3,2,1,0:T(8,128)} %broadcast_select_fusion), calls=%async_computation | async-start | bytes 8388608 | tf_op jit(solution)/shard_map/all_to_all | solution.py:55
  16.7 0.0 copy-done.4
  16.7 0.1 dynamic_slice.11
  16.8 0.6 fusion.24
  18.7 0.0 copy-done.2
  18.8 0.0 copy-done.3
  18.8 2.5 %conditional.6 = (f32[64,128,128]{1,2,0:T(8,128)}) conditional(s32[]{:T(128)} %convert_element_type.9, () %tuple.34, (f32[2,64,128,128]{3,2,1,0:T(8,128)}, f32[128,128]{1,0:T(8,128)S(1)}, f32[128,128]{1,0:T(8,128)S(1)}) %tuple.35), branch_computations={%region_5.6_spmd, %region_6.0_spmd} | conditional | flops 3221225472 | bytes 16908296 | solution.py:42
  18.8 2.4 %broadcast.55 = f32[64,128,128]{1,2,0:T(8,128)} broadcast(f32[]{:T(128)} %constant.18.clone), dimensions={} | broadcast | bytes 4194308 | tf_op jit(solution)/shard_map/broadcast.4
  21.2 0.0 copy-start.1
  21.2 0.0 copy-start.5
  21.3 2.5 %conditional.4 = (f32[64,128,128]{1,2,0:T(8,128)}) conditional(s32[]{:T(128)} %convert_element_type.8, () %tuple.30, (f32[2,64,128,128]{3,2,1,0:T(8,128)}, f32[128,128]{1,0:T(8,128)S(1)}, f32[128,128]{1,0:T(8,128)S(1)}) %tuple.31), branch_computations={%region_0.0_spmd, %region_1.0_spmd} | conditional | flops 3221225472 | bytes 16908296 | solution.py:42
  21.3 2.5 %broadcast.51 = f32[64,128,128]{1,2,0:T(8,128)} broadcast(f32[]{:T(128)} %constant.8.clone), dimensions={} | broadcast | bytes 4194308 | tf_op jit(solution)/shard_map/broadcast.2
  23.7 70.5 %all-to-all-done = f32[16,2,32,8,128]{4,3,2,1,0:T(8,128)} async-done(((f32[16,2,32,8,128]{4,3,2,1,0:T(8,128)}), f32[16,2,32,8,128]{4,3,2,1,0:T(8,128)}, u32[]{:S(2)}, u32[]{:S(2)}) %all-to-all-start) | async-done | bytes 4194336 | tf_op jit(solution)/shard_map/all_to_all | solution.py:55
  94.3 0.0 copy-done.1
  94.3 0.0 copy-done.5
  94.3 0.2 conditional.7
  94.5 0.2 conditional.5
  94.7 128.2 %psum.7 = f32[32,64]{1,0:T(8,128)} all-reduce(f32[32,64]{1,0:T(8,128)S(1)} %add.27), channel_id=1, replica_groups=mesh['group'=2,'module'=16] {'module'}, use_global_device_ids=true, to_apply=%region_10.11 | all-reduce | flops 2048 | bytes 16384 | tf_op jit(solution)/shard_map/psum | solution.py:72
  (5 shorter events, 0.0 us)
Async XLA Ops:
  0.0 1.6 copy-start
  9.1 7.6 %copy-start.4 = (s32[32]{0:T(128)S(1)}, s32[32]{0:T(128)}, u32[]{:S(2)}) copy-start(s32[32]{0:T(128)} %param.21) | copy-start | bytes 388
  9.1 9.6 %copy-start.2 = (f32[2,128,128]{2,1,0:T(8,128)S(1)}, f32[2,128,128]{2,1,0:T(8,128)}, u32[]{:S(2)}) copy-start(f32[2,128,128]{2,1,0:T(8,128)} %param.17) | copy-start | bytes 393220
  9.1 9.6 %copy-start.3 = (f32[2,128,128]{2,1,0:T(8,128)S(1)}, f32[2,128,128]{2,1,0:T(8,128)}, u32[]{:S(2)}) copy-start(f32[2,128,128]{2,1,0:T(8,128)} %param.18) | copy-start | bytes 393220
  9.1 85.1 %all-to-all-start = ((f32[16,2,32,8,128]{4,3,2,1,0:T(8,128)}), f32[16,2,32,8,128]{4,3,2,1,0:T(8,128)}, u32[]{:S(2)}, u32[]{:S(2)}) async-start(f32[16,2,32,8,128]{4,3,2,1,0:T(8,128)} %broadcast_select_fusion), calls=%async_computation | async-start | bytes 8388608 | tf_op jit(solution)/shard_map/all_to_all | solution.py:55
  21.2 73.0 %copy-start.1 = (f32[2,128,128]{2,1,0:T(8,128)S(1)}, f32[2,128,128]{2,1,0:T(8,128)}, u32[]{:S(2)}) copy-start(f32[2,128,128]{2,1,0:T(8,128)} %param.19) | copy-start | bytes 393220
  21.2 73.0 %copy-start.5 = (s32[16]{0:T(128)S(1)}, s32[16]{0:T(128)}, u32[]{:S(2)}) copy-start(s32[16]{0:T(128)} %param.20) | copy-start | bytes 196
where the time goes:
time: 224 us; the launch traced here: 223 us
  blocking collectives  128 us (57%)
  waiting for transfers between devices  70.5 us (31%)
  local copies, waits for them, and re-layouts  8.53 us (4%)
  starting transfers between devices  7.6 us (3%)
  other arithmetic  6.23 us (3%)
    psum x1, blocking collectives, body(): return lax.psum(running, 'module')  128 us
    all_to_all x1, waiting for transfers between devices, body(): lax.all_to_all(outgoing, 'module', split_axis=0, concat_axis=3, tiled=True)  70.5 us
    all_to_all x1, starting transfers between devices, body(): lax.all_to_all(outgoing, 'module', split_axis=0, concat_axis=3, tiled=True)  7.6 us
    another operation x4, local copies, waits for them, and re-layouts  4.93 us
    select_n x1, other arithmetic, body(): jnp.where(populated_slots[:, None, None, None], query_grads[safe_index],...  4.75 us
  transfers between devices with their start and end apart: 1, of which 1 were waited for; matrix products, arithmetic and copies ran while one was open for 3% of the time, Pallas kernels for 0%

commit v1 on v0

--- a/solution.py
+++ b/solution.py
@@ -2,6 +2,17 @@
 import jax.numpy as jnp
 from jax import lax
 from jax.sharding import PartitionSpec as P
+from jax.lax import all_to_all, axis_size
+
+enter_yards = lambda local: jnp.concatenate(
+    all_to_all(
+        jnp.stack(jnp.split(local, axis_size("module"), axis=0), 0),
+        axis_name="module",
+        split_axis=0,
+        concat_axis=0,
+    ),
+    axis=3,
+)
 
 
 def rotate(field, output_eigenbasis, inner_basis):
@@ -52,7 +63,7 @@
     populated_slots = slot_modules >= 0
     outgoing = jnp.where(populated_slots[:, None, None, None], query_grads[safe_index], 0.0)
     outgoing = outgoing.reshape((peer_count, slot_count) + outgoing.shape[1:])
-    received = lax.all_to_all(outgoing, "module", split_axis=0, concat_axis=3, tiled=True)[0]
+    received = enter_yards(outgoing)[0]
     running = jnp.zeros((query_count, example_count), jnp.float32)
     for number in range(slot_count):
         module = owned_modules[number]

time: 224 us -> 233 us (1.040)
  local copies, waits for them, and re-layouts: 8.53 us -> 20.1 us
    unnamed x12 -> x27, local copies, waits for them, and re-layouts: 0.06 us -> 11 us
    another operation x4 -> x5, local copies, waits for them, and re-layouts: 4.93 us -> 5.69 us
  transfers between devices with their start and end apart: 1 -> 1, of which waited for: 1 -> 1; matrix products, arithmetic and copies ran while one was open for 3% -> 2% of each run, Pallas kernels for 0% -> 0%
where the time goes in v1:
time: 233 us; the launch traced here: 232 us
  blocking collectives  128 us (55%)
  waiting for transfers between devices  70.5 us (30%)
  local copies, waits for them, and re-layouts  20.1 us (9%)
  starting transfers between devices  7.6 us (3%)
  other arithmetic  4.13 us (2%)
    psum x1, blocking collectives, body(): return lax.psum(running, 'module')  128 us
    all_to_all x1, waiting for transfers between devices, all_to_all(jnp.stack(jnp.split(local, axis_size('module'), axis=0), 0), a...  70.5 us
    unnamed x27, local copies, waits for them, and re-layouts  11 us
    all_to_all x1, starting transfers between devices, all_to_all(jnp.stack(jnp.split(local, axis_size('module'), axis=0), 0), a...  7.6 us
    another operation x4, local copies, waits for them, and re-layouts  4.93 us
  transfers between devices with their start and end apart: 1, of which 1 were waited for; matrix products, arithmetic and copies ran while one was open for 2% of the time, Pallas kernels for 0%

profile of v1, /device:TPU:0, one launch (start us, length us, event | category | flops | bytes accessed | tf_op | source)
XLA Modules:
  0.0 232.5 jit_solution(12734194429731628170)
XLA Ops:
  0.0 0.8 broadcast_maximum_fusion
  0.8 0.7 broadcast_compare_fusion
  1.5 0.1 copy-done
  1.6 2.8 %gather_fusion = f32[32,32,8,128]{3,2,1,0:T(8,128)} fusion(f32[16,32,8,128]{3,2,1,0:T(8,128)S(1)} %copy-done, s32[1024]{0:T(1024)S(1)} %pad_clamp_fusion), kind=kCustom, calls=%fused_computation | custom fusion | bytes 8388736 | tf_op jit(solution)/shard_map/gather | solution.py:64
  4.4 2.7 %broadcast_select_fusion = f32[32,32,8,128]{3,2,1,0:T(8,128)S(1)} fusion(f32[32,32,8,128]{3,2,1,0:T(8,128)} %gather_fusion, pred[32]{0:T(512)(128)(4,1)S(1)} %broadcast_compare_fusion), kind=kLoop, calls=%fused_computation.37 | loop fusion | flops 1048576 | bytes 8388640 | tf_op jit(solution)/shard_map/jit(_where)/select_n | solution.py:64
  7.0 0.7 fusion.39
  7.7 0.7 fusion.38
  8.5 0.7 fusion.37
  9.2 0.7 fusion.36
  9.9 0.7 fusion.35
  10.7 0.7 fusion.34
  11.4 0.7 fusion.33
  12.1 0.7 fusion.32
  12.8 0.7 fusion.31
  13.5 0.7 fusion.30
  14.3 0.7 fusion.29
  15.0 0.7 fusion.28
  15.7 0.7 fusion.27
  16.4 0.7 fusion.26
  17.1 0.7 fusion.25
  17.8 0.8 fusion.24
  18.6 7.6 %all-to-all-start = ((f32[16,1,2,32,8,128]{5,4,3,2,1,0:T(8,128)}), f32[16,1,2,32,8,128]{5,4,3,2,1,0:T(8,128)}, u32[]{:S(2)}, u32[]{:S(2)}) async-start(f32[16,1,2,32,8,128]{5,4,3,2,1,0:T(8,128)} %fusion.24), calls=%async_computation | async-start | bytes 8388608 | tf_op jit(solution)/shard_map/all_to_all | solution.py:8
  26.2 0.1 dynamic_slice.11
  26.3 0.6 fusion.40
  28.3 2.5 %conditional.6 = (f32[64,128,128]{1,2,0:T(8,128)}) conditional(s32[]{:T(128)} %convert_element_type.9, () %tuple.34, (f32[2,64,128,128]{3,2,1,0:T(8,128)}, f32[128,128]{1,0:T(8,128)S(1)}, f32[128,128]{1,0:T(8,128)S(1)}) %tuple.35), branch_computations={%region_5.6_spmd, %region_6.0_spmd} | conditional | flops 3221225472 | bytes 16908296 | solution.py:53
  28.3 2.4 %broadcast.54 = f32[64,128,128]{1,2,0:T(8,128)} broadcast(f32[]{:T(128)} %constant.18.clone), dimensions={} | broadcast | bytes 4194308 | tf_op jit(solution)/shard_map/broadcast.4
  30.7 2.5 %conditional.4 = (f32[64,128,128]{1,2,0:T(8,128)}) conditional(s32[]{:T(128)} %convert_element_type.8, () %tuple.30, (f32[2,64,128,128]{3,2,1,0:T(8,128)}, f32[128,128]{1,0:T(8,128)S(1)}, f32[128,128]{1,0:T(8,128)S(1)}) %tuple.31), branch_computations={%region_0.0_spmd, %region_1.0_spmd} | conditional | flops 3221225472 | bytes 16908296 | solution.py:53
  30.7 2.5 %broadcast.50 = f32[64,128,128]{1,2,0:T(8,128)} broadcast(f32[]{:T(128)} %constant.8.clone), dimensions={} | broadcast | bytes 4194308 | tf_op jit(solution)/shard_map/broadcast.2
  33.2 70.5 %all-to-all-done = f32[16,1,2,32,8,128]{5,4,3,2,1,0:T(8,128)} async-done(((f32[16,1,2,32,8,128]{5,4,3,2,1,0:T(8,128)}), f32[16,1,2,32,8,128]{5,4,3,2,1,0:T(8,128)}, u32[]{:S(2)}, u32[]{:S(2)}) %all-to-all-start) | async-done | bytes 4194336 | tf_op jit(solution)/shard_map/all_to_all | solution.py:8
  103.8 0.2 conditional.7
  104.0 0.2 conditional.5
  104.2 128.3 %psum.7 = f32[32,64]{1,0:T(8,128)} all-reduce(f32[32,64]{1,0:T(8,128)S(1)} %add.27), channel_id=1, replica_groups=mesh['group'=2,'module'=16] {'module'}, use_global_device_ids=true, to_apply=%region_10.11 | all-reduce | flops 2048 | bytes 16384 | tf_op jit(solution)/shard_map/psum | solution.py:83
  (16 shorter events, 0.1 us)
Async XLA Ops:
  0.0 1.6 copy-start
  18.6 7.6 %copy-start.4 = (s32[32]{0:T(128)S(1)}, s32[32]{0:T(128)}, u32[]{:S(2)}) copy-start(s32[32]{0:T(128)} %param.21) | copy-start | bytes 388
  18.6 9.6 %copy-start.2 = (f32[2,128,128]{2,1,0:T(8,128)S(1)}, f32[2,128,128]{2,1,0:T(8,128)}, u32[]{:S(2)}) copy-start(f32[2,128,128]{2,1,0:T(8,128)} %param.17) | copy-start | bytes 393220
  18.6 9.6 %copy-start.3 = (f32[2,128,128]{2,1,0:T(8,128)S(1)}, f32[2,128,128]{2,1,0:T(8,128)}, u32[]{:S(2)}) copy-start(f32[2,128,128]{2,1,0:T(8,128)} %param.18) | copy-start | bytes 393220
  18.6 85.1 %all-to-all-start = ((f32[16,1,2,32,8,128]{5,4,3,2,1,0:T(8,128)}), f32[16,1,2,32,8,128]{5,4,3,2,1,0:T(8,128)}, u32[]{:S(2)}, u32[]{:S(2)}) async-start(f32[16,1,2,32,8,128]{5,4,3,2,1,0:T(8,128)} %fusion.24), calls=%async_computation | async-start | bytes 8388608 | tf_op jit(solution)/shard_map/all_to_all | solution.py:8
  30.7 73.0 %copy-start.1 = (f32[2,128,128]{2,1,0:T(8,128)S(1)}, f32[2,128,128]{2,1,0:T(8,128)}, u32[]{:S(2)}) copy-start(f32[2,128,128]{2,1,0:T(8,128)} %param.19) | copy-start | bytes 393220
  30.7 73.0 %copy-start.5 = (s32[16]{0:T(128)S(1)}, s32[16]{0:T(128)}, u32[]{:S(2)}) copy-start(s32[16]{0:T(128)} %param.20) | copy-start | bytes 196

commit v2 on v0

--- a/solution.py
+++ b/solution.py
@@ -2,6 +2,10 @@
 import jax.numpy as jnp
 from jax import lax
 from jax.sharding import PartitionSpec as P
+
+
+def drive_node(chunk):
+    return jax.lax.all_gather(chunk, axis_name="module").sum(axis=0)
 
 
 def rotate(field, output_eigenbasis, inner_basis):
@@ -69,7 +73,7 @@
             keep_rank,
         )
         running = running + term
-    return lax.psum(running, "module")
+    return drive_node(running)
 
 
 def solution(mesh):

time: 224 us -> 184 us (0.82)
  blocking collectives: 128 us -> 88.5 us
    psum x1 -> x0, blocking collectives: 128 us -> none  [body(): return lax.psum(running, 'module')]
    all_gather x0 -> x1, blocking collectives: none -> 88.5 us  [drive_node(): return jax.lax.all_gather(chunk, axis_name='module').sum(axis=0)]
where the time goes in v2:
time: 184 us
  blocking collectives  88.5 us (48%)
  waiting for transfers between devices  70.5 us (38%)
  local copies, waits for them, and re-layouts  8.53 us (5%)
  starting transfers between devices  7.6 us (4%)
  other arithmetic  6.86 us (4%)
    all_gather x1, blocking collectives, drive_node(): return jax.lax.all_gather(chunk, axis_name='module').sum(axis=0)  88.5 us
    all_to_all x1, waiting for transfers between devices, body(): lax.all_to_all(outgoing, 'module', split_axis=0, concat_axis=3, tiled=True)  70.5 us
    all_to_all x1, starting transfers between devices, body(): lax.all_to_all(outgoing, 'module', split_axis=0, concat_axis=3, tiled=True)  7.6 us
    another operation x4, local copies, waits for them, and re-layouts  4.93 us
    select_n x1, other arithmetic, body(): jnp.where(populated_slots[:, None, None, None], query_grads[safe_index],...  4.75 us
  transfers between devices with their start and end apart: 1, of which 1 were waited for; matrix products, arithmetic and copies ran while one was open for 3% of the time, Pallas kernels for 0%

profile of v2, /device:TPU:0, one launch (start us, length us, event | category | flops | bytes accessed | tf_op | source)
XLA Modules:
  0.0 183.9 jit_solution(4197467513037245854)
XLA Ops:
  0.0 0.0 copy-start
  0.0 0.8 broadcast_maximum_fusion
  0.8 0.7 broadcast_compare_fusion
  1.5 0.1 broadcast_in_dim.24
  1.6 0.0 copy-done
  1.6 2.8 %gather_fusion = f32[32,32,8,128]{3,2,1,0:T(8,128)} fusion(f32[16,32,8,128]{3,2,1,0:T(8,128)S(1)} %copy-done, s32[1024]{0:T(1024)S(1)} %pad_clamp_fusion), kind=kCustom, calls=%fused_computation | custom fusion | bytes 8388736 | tf_op jit(solution)/shard_map/gather | solution.py:57
  4.4 4.8 %broadcast_select_fusion = f32[16,2,32,8,128]{4,3,2,1,0:T(8,128)} fusion(f32[16,2,32,8,128]{4,3,2,1,0:T(8,128)} %bitcast.81, pred[16,2]{1,0:T(8,128)(4,1)S(1)} %broadcast_in_dim.24), kind=kLoop, calls=%fused_computation.37 | loop fusion | flops 1048576 | bytes 8388640 | tf_op jit(solution)/shard_map/jit(_where)/select_n | solution.py:57
  9.1 0.0 copy-start.4
  9.1 0.0 copy-start.2
  9.1 0.0 copy-start.3
  9.1 7.6 %all-to-all-start = ((f32[16,2,32,8,128]{4,3,2,1,0:T(8,128)}), f32[16,2,32,8,128]{4,3,2,1,0:T(8,128)}, u32[]{:S(2)}, u32[]{:S(2)}) async-start(f32[16,2,32,8,128]{4,3,2,1,0:T(8,128)} %broadcast_select_fusion), calls=%async_computation | async-start | bytes 8388608 | tf_op jit(solution)/shard_map/all_to_all | solution.py:59
  16.7 0.0 copy-done.4
  16.7 0.1 dynamic_slice.11
  16.8 0.6 fusion.24
  18.7 0.0 copy-done.2
  18.8 0.0 copy-done.3
  18.8 2.5 %conditional.6 = (f32[64,128,128]{1,2,0:T(8,128)}) conditional(s32[]{:T(128)} %convert_element_type.9, () %tuple.34, (f32[2,64,128,128]{3,2,1,0:T(8,128)}, f32[128,128]{1,0:T(8,128)S(1)}, f32[128,128]{1,0:T(8,128)S(1)}) %tuple.35), branch_computations={%region_5.6_spmd, %region_6.0_spmd} | conditional | flops 3221225472 | bytes 16908296 | solution.py:46
  18.8 2.4 %broadcast.55 = f32[64,128,128]{1,2,0:T(8,128)} broadcast(f32[]{:T(128)} %constant.18.clone), dimensions={} | broadcast | bytes 4194308 | tf_op jit(solution)/shard_map/broadcast.4
  21.2 0.0 copy-start.1
  21.2 0.0 copy-start.5
  21.3 2.5 %conditional.4 = (f32[64,128,128]{1,2,0:T(8,128)}) conditional(s32[]{:T(128)} %convert_element_type.8, () %tuple.30, (f32[2,64,128,128]{3,2,1,0:T(8,128)}, f32[128,128]{1,0:T(8,128)S(1)}, f32[128,128]{1,0:T(8,128)S(1)}) %tuple.31), branch_computations={%region_0.0_spmd, %region_1.0_spmd} | conditional | flops 3221225472 | bytes 16908296 | solution.py:46
  21.3 2.5 %broadcast.51 = f32[64,128,128]{1,2,0:T(8,128)} broadcast(f32[]{:T(128)} %constant.8.clone), dimensions={} | broadcast | bytes 4194308 | tf_op jit(solution)/shard_map/broadcast.2
  23.7 70.5 %all-to-all-done = f32[16,2,32,8,128]{4,3,2,1,0:T(8,128)} async-done(((f32[16,2,32,8,128]{4,3,2,1,0:T(8,128)}), f32[16,2,32,8,128]{4,3,2,1,0:T(8,128)}, u32[]{:S(2)}, u32[]{:S(2)}) %all-to-all-start) | async-done | bytes 4194336 | tf_op jit(solution)/shard_map/all_to_all | solution.py:59
  94.3 0.0 copy-done.1
  94.3 0.0 copy-done.5
  94.3 0.2 conditional.7
  94.5 0.2 conditional.5
  94.7 88.5 %all-gather = f32[512,64]{1,0:T(8,128)S(1)} all-gather(f32[32,64]{1,0:T(8,128)S(1)} %add.25), channel_id=2, replica_groups=mesh['group'=2,'module'=16] {'module'}, dimensions={0}, use_global_device_ids=true | all-gather | bytes 139264 | tf_op jit(solution)/shard_map/all_gather | solution.py:8
  183.3 0.6 reduce_sum.27
  (5 shorter events, 0.0 us)
Async XLA Ops:
  0.0 1.6 copy-start
  9.1 7.6 %copy-start.4 = (s32[32]{0:T(128)S(1)}, s32[32]{0:T(128)}, u32[]{:S(2)}) copy-start(s32[32]{0:T(128)} %param.21) | copy-start | bytes 388
  9.1 9.6 %copy-start.2 = (f32[2,128,128]{2,1,0:T(8,128)S(1)}, f32[2,128,128]{2,1,0:T(8,128)}, u32[]{:S(2)}) copy-start(f32[2,128,128]{2,1,0:T(8,128)} %param.17) | copy-start | bytes 393220
  9.1 9.6 %copy-start.3 = (f32[2,128,128]{2,1,0:T(8,128)S(1)}, f32[2,128,128]{2,1,0:T(8,128)}, u32[]{:S(2)}) copy-start(f32[2,128,128]{2,1,0:T(8,128)} %param.18) | copy-start | bytes 393220
  9.1 85.1 %all-to-all-start = ((f32[16,2,32,8,128]{4,3,2,1,0:T(8,128)}), f32[16,2,32,8,128]{4,3,2,1,0:T(8,128)}, u32[]{:S(2)}, u32[]{:S(2)}) async-start(f32[16,2,32,8,128]{4,3,2,1,0:T(8,128)} %broadcast_select_fusion), calls=%async_computation | async-start | bytes 8388608 | tf_op jit(solution)/shard_map/all_to_all | solution.py:59
  21.2 73.0 %copy-start.1 = (f32[2,128,128]{2,1,0:T(8,128)S(1)}, f32[2,128,128]{2,1,0:T(8,128)}, u32[]{:S(2)}) copy-start(f32[2,128,128]{2,1,0:T(8,128)} %param.19) | copy-start | bytes 393220
  21.2 73.0 %copy-start.5 = (s32[16]{0:T(128)S(1)}, s32[16]{0:T(128)}, u32[]{:S(2)}) copy-start(s32[16]{0:T(128)} %param.20) | copy-start | bytes 196
